TPU v7x, 256 devices: a whole 4x4x8 slice. The times are simulated.
256 devices in a mesh: pipe: 8 (over x, core), seq: 8 (over z), tensor: 4 (over y).
Axes of the slice: x: 4, y: 4, z: 8, core: 2. Of those that a mesh axis runs over, the one named last changes fastest.
Arguments:
- hidden: bfloat16 [8, 1024, 14336], P('pipe', 'seq', 'tensor'), may hold values from -6 to 6
- down_weight: bfloat16 [8, 14336, 8192], P('pipe', 'tensor', 'seq'), may hold values from -0.046875 to 0.046875
- resid: bfloat16 [1024, 8192], P('tensor', 'seq'), may hold values from -42 to 42
- target: bfloat16 [1024, 8192], P('tensor', 'seq'), may hold values from -6 to 6
- gain: float32 [8192], P('seq'), may hold values from 0.1 to 1.9
- query_left: float32 [8, 8192, 32], P('pipe', 'seq'), may hold values from -0.0625 to 0.0625
- query_right: bfloat16 [8, 14336, 32], P('pipe', 'tensor'), may hold values from -0.046875 to 0.046875
- query_core: float32 [8, 1024], P('pipe'), may hold values from -6 to 6
- eigen: float32 [8, 1024], P('pipe'), may hold values from 0.1 to 10
- lengths: int32 [32], replicated, may hold values from 1 to 256, 1024 in all
Outputs:
- scores: float32 [32], P(('seq', 'tensor'))
All inputs are finite; a program needn't handle non-finite values.
Results may differ from a plain program's by a relative error of at most 0.0006.
Values may be sent and summed in bfloat16 or wider, within the bound.
No kernel may reach another device: no remote copies, remote signals or barrier semaphores. Data moves between devices by JAX's collectives and lax.ppermute only.
A program may use at most 64 MiB of HBM per device.

v0:
```python
import jax
import jax.numpy as jnp
from jax import lax
from jax.sharding import PartitionSpec as P

D = 8192


def per_device(
    hidden, down_weight, resid, target, gain, query_left, query_right, query_core, eigen, lengths
):
    tensor_count = lax.axis_size("tensor")
    gathered = lax.all_gather(hidden[0], "seq", axis=0, tiled=True)
    total_rows = gathered.shape[0]
    block_rows = total_rows // tensor_count
    weight = down_weight[0]
    right_partial = jnp.dot(gathered, query_right[0], preferred_element_type=jnp.float32)
    partial_value = lax.psum_scatter(
        jnp.dot(gathered, weight, preferred_element_type=jnp.float32).astype(jnp.bfloat16),
        "tensor",
        scatter_dimension=0,
        tiled=True,
    ).astype(jnp.float32)
    summed = lax.psum(partial_value, "pipe")
    stream = resid.astype(jnp.float32) + summed
    weighted_target = gain[None, :] * target.astype(jnp.float32)
    square_sum, inner = lax.psum(
        (jnp.sum(stream * stream, axis=1), jnp.sum(weighted_target * stream, axis=1)), "seq"
    )
    root = jnp.sqrt(square_sum / D + 1e-05)
    grad_stream = (
        weighted_target / root[:, None] - stream * (inner / (D * root * root * root))[:, None]
    )
    left_proj = jnp.dot(grad_stream, query_left[0], precision=lax.Precision.HIGHEST)
    right_proj = lax.psum_scatter(right_partial, "tensor", scatter_dimension=0, tiled=True)
    rank_width = left_proj.shape[1]
    outer = (left_proj[:, :, None] * right_proj[:, None, :]).reshape(
        block_rows, rank_width * rank_width
    )
    ends = jnp.cumsum(lengths)
    starts = ends - lengths
    token = lax.axis_index("tensor") * block_rows + jnp.arange(block_rows, dtype=jnp.int32)
    member = ((token[None, :] >= starts[:, None]) & (token[None, :] < ends[:, None])).astype(
        jnp.float32
    )
    partial_cores = jnp.dot(member, outer, precision=lax.Precision.HIGHEST)
    cores = lax.psum_scatter(partial_cores, ("seq", "tensor"), scatter_dimension=0, tiled=True)
    scaled = cores / eigen[0][None, :]
    score_term = jnp.sum(query_core[0][None, :] * scaled, axis=1)
    self_term = jnp.sum(cores * scaled, axis=1)
    score_total, self_total = lax.psum((score_term, self_term), "pipe")
    return score_total / jnp.sqrt(self_total + 1e-06)


def solution(mesh):
    placed = (
        P("pipe", "seq", "tensor"),
        P("pipe", "tensor", "seq"),
        P("tensor", "seq"),
        P("tensor", "seq"),
        P("seq"),
        P("pipe", "seq", None),
        P("pipe", "tensor", None),
        P("pipe", None),
        P("pipe", None),
        P(),
    )
    return jax.shard_map(
        per_device, mesh=mesh, in_specs=placed, out_specs=P(("seq", "tensor")), check_vma=False
    )
```

profile of v0, /device:TPU:1, one launch (start us, length us, event | category | flops | bytes accessed | tf_op | source)
XLA Modules:
  0.0 375.0 jit_solution(16374362809391073880)
XLA Ops:
  6.5 0.0 copy-start
  6.5 0.0 all-gather.3.cloned.1.call-start
  6.5 0.7 all-gather.3.cloned.1.call-update
  7.3 0.0 copy-start.6
  7.3 0.0 reduce-scatter.3.cloned.1.call-start
  7.3 90.0 %all-gather.3.cloned.1.call-done = bf16[1,1024,3584]{2,1,0:T(8,128)(2,1)} async-done(((bf16[1,128,3584]{2,1,0:T(8,128)(2,1)}), bf16[1,1024,3584]{2,1,0:T(8,128)(2,1)}) %all-gather.3.cloned.1.call-update) | async-done | bytes 7340048 | tf_op jit(solution)/shard_map/all_gather | solution.py:13
  97.3 13.3 %fusion.5 = bf16[1024,1024]{1,0:T(8,128)(2,1)} fusion(bf16[1,3584,1024]{2,1,0:T(8,128)(2,1)} %param.11, bf16[1,1024,3584]{2,1,0:T(8,128)(2,1)} %all-gather.3.cloned.1.call-done), kind=kOutput, calls=%fused_computation.5 | convolution fusion | flops 7517241344 | bytes 16777216 | tf_op jit(solution)/shard_map/dot_general | solution.py:19
  110.6 0.0 copy-start.1
  110.6 0.0 copy-start.2
  110.6 0.0 copy-start.3
  110.6 0.0 copy-start.7
  110.6 0.0 reduce-scatter.3.cloned.1.call-update
  110.6 0.0 reduce-scatter.5.cloned.1.call-start
  110.7 0.0 copy-done.6
  110.7 0.1 copy.15
  110.8 0.1 reduce-window.8
  110.8 0.1 reduce.2
  111.0 0.0 copy-done
  111.0 6.0 %fusion.2 = f32[1024,32]{0,1:T(8,128)} fusion(bf16[1,1024,3584]{2,1,0:T(8,128)(2,1)} %all-gather.3.cloned.1.call-done, bf16[1,3584,32]{1,2,0:T(8,128)(2,1)S(1)} %copy-done), kind=kOutput, calls=%fused_computation.2 | convolution fusion | flops 234881024 | bytes 7700480 | tf_op jit(solution)/shard_map/dot_general | solution.py:17
  116.9 0.0 copy-start.8
  116.9 0.0 copy-start.4
  116.9 0.0 copy-start.5
  116.9 0.0 reduce-scatter.5.cloned.1.call-update
  117.0 0.0 all-reduce.6.cloned.1.call-start
  117.0 24.6 %reduce-scatter.3.cloned.1.call-done = bf16[256,1024]{1,0:T(8,128)(2,1)} async-done(((bf16[1024,1024]{1,0:T(8,128)(2,1)}), bf16[256,1024]{1,0:T(8,128)(2,1)}) %reduce-scatter.3.cloned.1.call-update) | async-done | bytes 524304 | tf_op jit(solution)/shard_map/reduce_scatter | solution.py:18
  141.7 50.4 %all-reduce.7 = f32[256,1024]{1,0:T(8,128)S(1)} all-reduce(bf16[256,1024]{1,0:T(8,128)(2,1)} %reduce-scatter.3.cloned.1.call-done), channel_id=1, replica_groups=mesh['pipe'=8,'seq'=8,'tensor'=4] {'pipe'}, use_global_device_ids=true, to_apply=%region_2.0 | all-reduce | flops 262144 | bytes 1572864 | tf_op jit(solution)/shard_map/psum | solution.py:24
  192.1 0.0 copy-done.1
  192.1 0.0 copy-done.2
  192.1 0.0 copy-done.3
  192.1 0.4 multiply_reduce_fusion.1
  192.5 13.7 %all-reduce.1 = (f32[256]{0:T(256)S(1)}, f32[256]{0:T(256)S(1)}) all-reduce(f32[256]{0:T(256)S(1)} %get-tuple-element.6, f32[256]{0:T(256)S(1)} %get-tuple-element.5), channel_id=1, replica_groups=mesh['pipe'=8,'seq'=8,'tensor'=4] {'seq'}, use_global_device_ids=true, to_apply=%region_6.0 | all-reduce | flops 512 | bytes 4096 | tf_op jit(solution)/shard_map/psum | solution.py:27
  206.2 0.0 copy-done.7
  206.2 1.2 fusion.10
  207.4 0.0 reduce-scatter.5.cloned.1.call-done
  207.5 0.9 broadcast_multiply_fusion
  208.3 1.3 fusion.19
  209.6 0.0 all-reduce.6.cloned.1.call-update
  209.7 0.0 copy-done.8
  209.7 0.6 dynamic-slice
  210.3 137.4 %all-reduce.6.cloned.1.call-done = f32[32,1024]{1,0:T(8,128)} async-done(((f32[32,1024]{1,0:T(8,128)}), f32[32,1024]{1,0:T(8,128)}) %all-reduce.6.cloned.1.call-update) | async-done | bytes 131088
  347.7 0.0 copy-done.4
  347.7 0.0 copy-done.5
  347.7 2.0 multiply_reduce_fusion.2
  349.7 16.9 %all-reduce.2 = (f32[1]{0:T(128)}, f32[1]{0:T(128)}) all-reduce(f32[1]{0:T(128)} %bitcast.6, f32[1]{0:T(128)} %bitcast.7), channel_id=1, replica_groups=mesh['pipe'=8,'seq'=8,'tensor'=4] {'pipe'}, use_global_device_ids=true, to_apply=%region_10.11 | all-reduce | flops 2 | bytes 16 | tf_op jit(solution)/shard_map/psum | solution.py:51
  (3 shorter events, 0.0 us)
Async XLA Ops:
  6.5 104.4 %copy-start = (bf16[1,3584,32]{1,2,0:T(8,128)(2,1)S(1)}, bf16[1,3584,32]{1,2,0:T(8,128)(2,1)}, u32[]{:S(2)}) copy-start(bf16[1,3584,32]{1,2,0:T(8,128)(2,1)} %param.16) | copy-start | bytes 688132
  6.5 90.8 %all-gather.3.cloned.1.call-start = ((), (), s32[]{:S(2)}) async-start(), calls=%async_computation.4 | async-start | bytes 8257536 | tf_op jit(solution)/shard_map/all_gather | solution.py:13
  7.3 103.4 %copy-start.6 = (s32[32]{0:T(128)S(1)}, s32[32]{0:T(128)}, u32[]{:S(2)}) copy-start(s32[32]{0:T(128)} %param.19) | copy-start | bytes 388
  7.3 134.4 %reduce-scatter.3.cloned.1.call-start = ((), (), s32[]{:S(2)}) async-start(), calls=%async_computation.2 | async-start | bytes 2621440 | tf_op jit(solution)/shard_map/reduce_scatter | solution.py:18
  110.6 81.5 %copy-start.1 = (bf16[256,1024]{1,0:T(8,128)(2,1)S(1)}, bf16[256,1024]{1,0:T(8,128)(2,1)}, u32[]{:S(2)}) copy-start(bf16[256,1024]{1,0:T(8,128)(2,1)} %param.13) | copy-start | bytes 1572868
  110.6 81.5 %copy-start.2 = (bf16[256,1024]{1,0:T(8,128)(2,1)S(1)}, bf16[256,1024]{1,0:T(8,128)(2,1)}, u32[]{:S(2)}) copy-start(bf16[256,1024]{1,0:T(8,128)(2,1)} %param.12) | copy-start | bytes 1572868
  110.6 81.5 %copy-start.3 = (f32[1024]{0:T(1024)S(1)}, f32[1024]{0:T(1024)}, u32[]{:S(2)}) copy-start(f32[1024]{0:T(1024)} %param.14) | copy-start | bytes 12292
  110.6 95.6 %copy-start.7 = (f32[1,1024,32]{1,2,0:T(8,128)S(1)}, f32[1,1024,32]{1,2,0:T(8,128)}, u32[]{:S(2)}) copy-start(f32[1,1024,32]{1,2,0:T(8,128)} %param.15) | copy-start | bytes 393220
  110.6 96.9 %reduce-scatter.5.cloned.1.call-start = ((), (), s32[]{:S(2)}) async-start(), calls=%async_computation.3 | async-start | bytes 163840 | tf_op jit(solution)/shard_map/reduce_scatter | solution.py:35
  116.9 92.8 %copy-start.8 = (u32[256]{0:T(256)S(1)}, u32[256]{0:T(256)}, u32[]{:S(2)}) copy-start(u32[256]{0:T(256)} %constant.28) | copy-start | bytes 3076
  116.9 230.7 %copy-start.4 = (f32[1,1024]{1,0:T(1,128)S(1)}, f32[1,1024]{1,0:T(1,128)}, u32[]{:S(2)}) copy-start(f32[1,1024]{1,0:T(1,128)} %param.17) | copy-start | bytes 12292
  116.9 230.7 %copy-start.5 = (f32[1,1024]{1,0:T(1,128)S(1)}, f32[1,1024]{1,0:T(1,128)}, u32[]{:S(2)}) copy-start(f32[1,1024]{1,0:T(1,128)} %param.18) | copy-start | bytes 12292
  117.0 230.7 %all-reduce.6.cloned.1.call-start = ((), (), s32[]{:S(2)}) async-start(), calls=%async_computation.5 | async-start | bytes 262144
Sparse Core Ops, SparseCore 0:
  9.1 88.1 all-gather.2
  110.7 30.8 reduce-scatter.2
  144.3 20.4 reduce-scatter.4
  209.8 137.8 all-reduce.5
where the time goes:
time: 375 us
  waiting for transfers between devices  253 us (67%)
  blocking collectives  81 us (22%)
  matrix products  21.7 us (6%)
  between operations  15.1 us (4%)
    unnamed x5, waiting for transfers between devices  138 us
    all_gather x1, waiting for transfers between devices, per_device(): gathered = lax.all_gather(hidden[0], 'seq', axis=0, tiled=True)  90 us
    psum x1, blocking collectives, per_device(): summed = lax.psum(partial_value, 'pipe')  50.4 us
    reduce_scatter x1, waiting for transfers between devices, per_device(): lax.psum_scatter(jnp.dot(gathered, weight, preferred_element_type=jnp.flo...  24.6 us
    psum x1, blocking collectives, per_device(): score_total, self_total = lax.psum((score_term, self_term), 'pipe')  16.9 us
    psum x1, blocking collectives, per_device(): lax.psum((jnp.sum(stream * stream, axis=1), jnp.sum(weighted_target * str...  13.7 us
    dot_general x1, matrix products, per_device(): jnp.dot(gathered, weight, preferred_element_type=jnp.float32)  13.3 us
  transfers between devices with their start and end apart: 4, of which 3 were waited for; matrix products, arithmetic and copies ran while one was open for 2% of the time, Pallas kernels for 0%

commit v1 on v0

--- a/solution.py
+++ b/solution.py
@@ -10,7 +10,9 @@
     hidden, down_weight, resid, target, gain, query_left, query_right, query_core, eigen, lengths
 ):
     tensor_count = lax.axis_size("tensor")
-    gathered = lax.all_gather(hidden[0], "seq", axis=0, tiled=True)
+    gathered = jnp.concatenate(
+        lax.all_to_all(jnp.stack([hidden[0]] * lax.axis_size("seq")), "seq", 0, 0), axis=0
+    )
     total_rows = gathered.shape[0]
     block_rows = total_rows // tensor_count
     weight = down_weight[0]

time: 375 us -> 456 us (1.22)
  blocking collectives: 81 us -> 252 us
  waiting for transfers between devices: 253 us -> 162 us
  local copies, waits for them, and re-layouts: 0.71 us -> 5.63 us
    all_to_all x0 -> x1, blocking collectives: none -> 171 us  [per_device(): lax.all_to_all(jnp.stack([hidden[0]] * lax.axis_size('seq')), 'seq', 0, 0)]
    all_gather x1 -> x0, waiting for transfers between devices: 90 us -> none  [per_device(): gathered = lax.all_gather(hidden[0], 'seq', axis=0, tiled=True)]
    unnamed x5 -> x4, waiting for transfers between devices: 138 us -> 137 us
  transfers between devices with their start and end apart: 4 -> 3, of which waited for: 3 -> 2; matrix products, arithmetic and copies ran while one was open for 2% -> 2% of each run, Pallas kernels for 0% -> 0%
where the time goes in v1:
time: 456 us
  blocking collectives  252 us (55%)
  waiting for transfers between devices  162 us (36%)
  matrix products  17.5 us (4%)
  between operations  15.1 us (3%)
  local copies, waits for them, and re-layouts  5.63 us (1%)
    all_to_all x1, blocking collectives, per_device(): lax.all_to_all(jnp.stack([hidden[0]] * lax.axis_size('seq')), 'seq', 0, 0)  171 us
    unnamed x4, waiting for transfers between devices  137 us
    psum x1, blocking collectives, per_device(): summed = lax.psum(partial_value, 'pipe')  50.4 us
    reduce_scatter x1, waiting for transfers between devices, per_device(): lax.psum_scatter(jnp.dot(gathered, weight, preferred_element_type=jnp.flo...  24.2 us
    psum x1, blocking collectives, per_device(): score_total, self_total = lax.psum((score_term, self_term), 'pipe')  16.9 us
    psum x1, blocking collectives, per_device(): lax.psum((jnp.sum(stream * stream, axis=1), jnp.sum(weighted_target * str...  13.7 us
  transfers between devices with their start and end apart: 3, of which 2 were waited for; matrix products, arithmetic and copies ran while one was open for 2% of the time, Pallas kernels for 0%

profile of v1, /device:TPU:1, one launch (start us, length us, event | category | flops | bytes accessed | tf_op | source)
XLA Modules:
  0.0 455.6 jit_solution(6347826501617459759)
XLA Ops:
  6.5 0.0 copy-start
  6.5 0.0 reduce-scatter.3.cloned.1.call-start
  6.5 0.0 slice-start
  6.5 1.9 stack.3
  8.5 0.0 slice-start.1
  8.5 171.1 %all_to_all.5 = bf16[8,128,3584]{2,1,0:T(8,128)(2,1)S(1)} all-to-all(bf16[8,128,3584]{2,1,0:T(8,128)(2,1)S(1)} %stack.3), channel_id=1, replica_groups=mesh['pipe'=8,'seq'=8,'tensor'=4] {'seq'}, dimensions={0} | all-to-all | bytes 14680064 | tf_op jit(solution)/shard_map/all_to_all | solution.py:14
  179.6 3.0 copy-done.1
  182.6 0.0 slice-done
  182.6 0.0 slice-done.1
  182.6 0.0 copy-start.7
  182.6 9.0 %fusion.2 = bf16[1024,1024]{1,0:T(8,128)(2,1)} fusion(bf16[1024,3584]{1,0:T(8,128)(2,1)S(1)} %bitcast.21, bf16[1,3584,1024]{2,1,0:T(8,128)(2,1)S(1)} %bitcast.27), kind=kOutput, calls=%fused_computation.2 | convolution fusion | flops 7517241344 | bytes 16777216 | tf_op jit(solution)/shard_map/dot_general | solution.py:21
  191.6 0.0 copy-start.2
  191.6 0.0 copy-start.3
  191.6 0.0 copy-start.4
  191.6 0.0 copy-start.8
  191.6 0.0 reduce-scatter.3.cloned.1.call-update
  191.6 0.0 reduce-scatter.5.cloned.1.call-start
  191.7 0.0 copy-done.7
  191.7 0.1 copy.15
  191.8 0.1 reduce-window.8
  191.9 0.1 reduce.2
  192.0 0.0 copy-done
  192.0 6.0 %fusion.12 = f32[1024,32]{0,1:T(8,128)} fusion(bf16[1024,3584]{1,0:T(8,128)(2,1)} %bitcast.22, bf16[1,3584,32]{1,2,0:T(8,128)(2,1)S(1)} %copy-done), kind=kOutput, calls=%fused_computation.15 | convolution fusion | flops 234881024 | bytes 7700480 | tf_op jit(solution)/shard_map/dot_general | solution.py:19
  198.0 0.0 copy-start.9
  198.0 0.0 copy-start.5
  198.0 0.0 copy-start.6
  198.0 0.0 reduce-scatter.5.cloned.1.call-update
  198.0 0.0 all-reduce.6.cloned.1.call-start
  198.0 24.2 %reduce-scatter.3.cloned.1.call-done = bf16[256,1024]{1,0:T(8,128)(2,1)} async-done(((bf16[1024,1024]{1,0:T(8,128)(2,1)}), bf16[256,1024]{1,0:T(8,128)(2,1)}) %reduce-scatter.3.cloned.1.call-update) | async-done | bytes 524304 | tf_op jit(solution)/shard_map/reduce_scatter | solution.py:20
  222.2 50.4 %all-reduce.7 = f32[256,1024]{1,0:T(8,128)S(1)} all-reduce(bf16[256,1024]{1,0:T(8,128)(2,1)} %reduce-scatter.3.cloned.1.call-done), channel_id=1, replica_groups=mesh['pipe'=8,'seq'=8,'tensor'=4] {'pipe'}, use_global_device_ids=true, to_apply=%region_2.0 | all-reduce | flops 262144 | bytes 1572864 | tf_op jit(solution)/shard_map/psum | solution.py:26
  272.7 0.0 copy-done.2
  272.7 0.0 copy-done.3
  272.7 0.0 copy-done.4
  272.7 0.4 multiply_reduce_fusion.1
  273.0 13.7 %all-reduce.1 = (f32[256]{0:T(256)S(1)}, f32[256]{0:T(256)S(1)}) all-reduce(f32[256]{0:T(256)S(1)} %get-tuple-element.6, f32[256]{0:T(256)S(1)} %get-tuple-element.5), channel_id=1, replica_groups=mesh['pipe'=8,'seq'=8,'tensor'=4] {'seq'}, use_global_device_ids=true, to_apply=%region_6.0 | all-reduce | flops 512 | bytes 4096 | tf_op jit(solution)/shard_map/psum | solution.py:29
  286.8 0.0 copy-done.8
  286.8 1.2 fusion.5
  288.0 0.0 reduce-scatter.5.cloned.1.call-done
  288.0 0.9 broadcast_multiply_fusion
  288.9 1.3 fusion.15
  290.2 0.0 all-reduce.6.cloned.1.call-update
  290.2 0.0 copy-done.9
  290.2 0.6 dynamic-slice
  290.8 137.4 %all-reduce.6.cloned.1.call-done = f32[32,1024]{1,0:T(8,128)} async-done(((f32[32,1024]{1,0:T(8,128)}), f32[32,1024]{1,0:T(8,128)}) %all-reduce.6.cloned.1.call-update) | async-done | bytes 131088
  428.2 0.0 copy-done.5
  428.3 0.0 copy-done.6
  428.3 2.0 multiply_reduce_fusion.2
  430.3 16.9 %all-reduce.2 = (f32[1]{0:T(128)}, f32[1]{0:T(128)}) all-reduce(f32[1]{0:T(128)} %bitcast.7, f32[1]{0:T(128)} %bitcast.8), channel_id=1, replica_groups=mesh['pipe'=8,'seq'=8,'tensor'=4] {'pipe'}, use_global_device_ids=true, to_apply=%region_10.11 | all-reduce | flops 2 | bytes 16 | tf_op jit(solution)/shard_map/psum | solution.py:53
  (5 shorter events, 0.0 us)
Async XLA Ops:
  6.5 185.5 %copy-start = (bf16[1,3584,32]{1,2,0:T(8,128)(2,1)S(1)}, bf16[1,3584,32]{1,2,0:T(8,128)(2,1)}, u32[]{:S(2)}) copy-start(bf16[1,3584,32]{1,2,0:T(8,128)(2,1)} %param.16) | copy-start | bytes 688132
  6.5 215.7 %reduce-scatter.3.cloned.1.call-start = ((), (), s32[]{:S(2)}) async-start(), calls=%async_computation.3 | async-start | bytes 2621440 | tf_op jit(solution)/shard_map/reduce_scatter | solution.py:20
  6.5 176.1 %slice-start = ((s8[7340032]{0:T(1024)(128)(4,1)}), s8[4194304]{0:T(1024)(128)(4,1)S(1)}, s32[]{:S(2)}) async-start(s8[7340032]{0:T(1024)(128)(4,1)} %bitcast.26), calls=%async_computation.6 | async-start | bytes 8388608
  8.5 174.1 %slice-start.1 = ((s8[7340032]{0:T(1024)(128)(4,1)}), s8[3145728]{0:T(1024)(128)(4,1)S(1)}, s32[]{:S(2)}) async-start(s8[7340032]{0:T(1024)(128)(4,1)} %bitcast.26), calls=%async_computation.7 | async-start | bytes 6291456
  179.6 3.0 copy-start.1
  182.6 9.1 %copy-start.7 = (s32[32]{0:T(128)S(1)}, s32[32]{0:T(128)}, u32[]{:S(2)}) copy-start(s32[32]{0:T(128)} %param.19) | copy-start | bytes 388
  191.6 81.0 %copy-start.2 = (bf16[256,1024]{1,0:T(8,128)(2,1)S(1)}, bf16[256,1024]{1,0:T(8,128)(2,1)}, u32[]{:S(2)}) copy-start(bf16[256,1024]{1,0:T(8,128)(2,1)} %param.13) | copy-start | bytes 1572868
  191.6 81.1 %copy-start.3 = (bf16[256,1024]{1,0:T(8,128)(2,1)S(1)}, bf16[256,1024]{1,0:T(8,128)(2,1)}, u32[]{:S(2)}) copy-start(bf16[256,1024]{1,0:T(8,128)(2,1)} %param.12) | copy-start | bytes 1572868
  191.6 81.1 %copy-start.4 = (f32[1024]{0:T(1024)S(1)}, f32[1024]{0:T(1024)}, u32[]{:S(2)}) copy-start(f32[1024]{0:T(1024)} %param.14) | copy-start | bytes 12292
  191.6 95.2 %copy-start.8 = (f32[1,1024,32]{1,2,0:T(8,128)S(1)}, f32[1,1024,32]{1,2,0:T(8,128)}, u32[]{:S(2)}) copy-start(f32[1,1024,32]{1,2,0:T(8,128)} %param.15) | copy-start | bytes 393220
  191.6 96.4 %reduce-scatter.5.cloned.1.call-start = ((), (), s32[]{:S(2)}) async-start(), calls=%async_computation.4 | async-start | bytes 163840 | tf_op jit(solution)/shard_map/reduce_scatter | solution.py:37
  198.0 92.3 %copy-start.9 = (u32[256]{0:T(256)S(1)}, u32[256]{0:T(256)}, u32[]{:S(2)}) copy-start(u32[256]{0:T(256)} %constant.28) | copy-start | bytes 3076
  198.0 230.3 %copy-start.5 = (f32[1,1024]{1,0:T(1,128)S(1)}, f32[1,1024]{1,0:T(1,128)}, u32[]{:S(2)}) copy-start(f32[1,1024]{1,0:T(1,128)} %param.17) | copy-start | bytes 12292
  198.0 230.3 %copy-start.6 = (f32[1,1024]{1,0:T(1,128)S(1)}, f32[1,1024]{1,0:T(1,128)}, u32[]{:S(2)}) copy-start(f32[1,1024]{1,0:T(1,128)} %param.18) | copy-start | bytes 12292
  198.0 230.3 %all-reduce.6.cloned.1.call-start = ((), (), s32[]{:S(2)}) async-start(), calls=%async_computation.5 | async-start | bytes 262144
Sparse Core Ops, SparseCore 0:
  191.8 30.4 reduce-scatter.2
  224.9 20.5 reduce-scatter.4
  290.4 137.8 all-reduce.5
